TPU v7x, 32 devices: a whole 2x2x4 slice. The times are simulated.
32 devices in a mesh: wide: 16 (over z, x, core), narrow: 2 (over y).
Axes of the slice: x: 2, y: 2, z: 4, core: 2. Of those that a mesh axis runs over, the one named last changes fastest.
Arguments:
- query_rows: bfloat16 [640, 6144], P('wide', 'narrow'), may hold values from -30 to 30
- key_rows: bfloat16 [640, 6144], P('wide', 'narrow'), may hold values from -10 to 10
- value_rows: bfloat16 [640, 6144], P('wide', 'narrow'), may hold values from -6 to 6
- mid_grad: bfloat16 [5120, 2048], P(('wide', 'narrow')), may hold values from -6 to 6
- link_weight: bfloat16 [768, 2048], replicated, may hold values from -0.21875 to 0.21875
Outputs:
- query_grad: bfloat16 [640, 6144], P('wide', 'narrow')
- key_grad: bfloat16 [640, 6144], P('wide', 'narrow')
- value_grad: bfloat16 [640, 6144], P('wide', 'narrow')
All inputs are finite; a program needn't handle non-finite values.
Results may differ from a plain program's by a relative error of at most 0.0066.
Values may be sent and summed in bfloat16 or wider, within the bound.
No kernel may reach another device: no remote copies, remote signals or barrier semaphores. Data moves between devices by JAX's collectives and lax.ppermute only.
A program may use at most 64 MiB of HBM per device.

v0:
```python
import math
import jax
import jax.numpy as jnp
from jax import lax
from jax.sharding import PartitionSpec as P

HD = 128
PATCH = 8
lowest = -1e30


def on_device(query_rows, key_rows, value_rows, mid_grad, link_weight):
    groups = lax.axis_size("narrow")
    patches = query_rows.shape[0]
    columns = query_rows.shape[1]
    heads_here = columns // HD
    scaling = 1.0 / math.sqrt(HD)
    local_patches = mid_grad.shape[0] // PATCH
    grouped = mid_grad.reshape(local_patches, groups, PATCH // groups, mid_grad.shape[1])
    moved = jnp.einsum(
        "abcm,pm->abcp",
        lax.all_to_all(grouped, "narrow", split_axis=1, concat_axis=0, tiled=True),
        link_weight,
        preferred_element_type=jnp.float32,
    ).astype(jnp.bfloat16)
    incoming = moved.reshape(patches, columns)
    incoming_heads = incoming.reshape(patches, heads_here, HD)
    query_heads = query_rows.reshape(patches, heads_here, HD)
    key_heads = key_rows.reshape(patches, heads_here, HD)
    value_heads = value_rows.reshape(patches, heads_here, HD)
    own_pos = lax.axis_index("wide") * patches + jnp.arange(patches, dtype=jnp.int32)
    total_rows = patches * lax.axis_size("wide")
    empty_store = jnp.zeros((total_rows, columns), jnp.bfloat16)
    fold_start = (
        jnp.full((heads_here, patches), lowest, jnp.float32),
        jnp.zeros((heads_here, patches), jnp.float32),
        jnp.zeros((heads_here, patches), jnp.float32),
        empty_store,
        empty_store,
    )
    pieces = (
        lax.all_gather(key_rows, "wide", axis=0, tiled=True),
        lax.all_gather(value_rows, "wide", axis=0, tiled=True),
    )
    key_piece, value_piece = pieces
    piece_rows = key_piece.shape[0]
    key_split = key_piece.reshape(piece_rows, heads_here, HD)
    value_split = value_piece.reshape(piece_rows, heads_here, HD)
    piece_pos = jnp.arange(piece_rows, dtype=jnp.int32)
    allowed = piece_pos[None, None, :] <= own_pos[None, :, None]
    scores = (
        jnp.einsum("qhd,khd->hqk", query_heads, key_split, preferred_element_type=jnp.float32)
        * scaling
    )
    scores = jnp.where(allowed, scores, lowest)
    products = jnp.einsum(
        "qhd,khd->hqk", incoming_heads, value_split, preferred_element_type=jnp.float32
    )
    old_max, old_total, old_tilt = fold_start[:3]
    new_max = jnp.maximum(old_max, jnp.max(scores, axis=2))
    expo = jnp.where(allowed, jnp.exp(scores - new_max[:, :, None]), 0.0)
    stats = (new_max, jnp.sum(expo, axis=2), jnp.sum(expo * products, axis=2))
    key_store = pieces[0]
    value_store = pieces[1]
    folded = stats + (key_store, value_store)
    run_max, run_total, run_tilt = (folded[0], folded[1], folded[2])
    log_total = run_max + jnp.log(run_total)
    row_delta = run_tilt / run_total
    key_all = folded[3].reshape(total_rows, heads_here, HD)
    value_all = folded[4].reshape(total_rows, heads_here, HD)
    every_pos = jnp.arange(total_rows, dtype=jnp.int32)
    allowed_q = every_pos[None, None, :] <= own_pos[None, :, None]
    scores_q = (
        jnp.einsum("qhd,khd->hqk", query_heads, key_all, preferred_element_type=jnp.float32)
        * scaling
    )
    products_q = jnp.einsum(
        "qhd,khd->hqk", incoming_heads, value_all, preferred_element_type=jnp.float32
    )
    weights_q = jnp.where(
        allowed_q, jnp.exp(jnp.where(allowed_q, scores_q, lowest) - log_total[:, :, None]), 0.0
    )
    score_grad_q = (weights_q * (products_q - row_delta[:, :, None])).astype(jnp.bfloat16)
    query_accum = jnp.einsum(
        "hqk,khd->qhd", score_grad_q, key_all, preferred_element_type=jnp.float32
    )
    query_grad = (query_accum * scaling).astype(jnp.bfloat16).reshape(patches, columns)
    total_all, delta_all = (
        lax.all_gather(log_total, "wide", axis=1, tiled=True),
        lax.all_gather(row_delta, "wide", axis=1, tiled=True),
    )
    query_piece = lax.all_gather(query_rows, "wide", axis=0, tiled=True)
    grad_piece = lax.all_gather(incoming, "wide", axis=0, tiled=True)
    piece_rows = query_piece.shape[0]
    query_split = query_piece.reshape(piece_rows, heads_here, HD)
    grad_split = grad_piece.reshape(piece_rows, heads_here, HD)
    piece_pos = jnp.arange(piece_rows, dtype=jnp.int32)
    allowed = own_pos[None, None, :] <= piece_pos[None, :, None]
    scores = (
        jnp.einsum("qhd,khd->hqk", query_split, key_heads, preferred_element_type=jnp.float32)
        * scaling
    )
    scores = jnp.where(allowed, scores, lowest)
    products = jnp.einsum(
        "qhd,khd->hqk", grad_split, value_heads, preferred_element_type=jnp.float32
    )
    weights = jnp.where(allowed, jnp.exp(scores - total_all[:, :, None]), 0.0)
    score_grad = (weights * (products - delta_all[:, :, None])).astype(jnp.bfloat16)
    key_accum = jnp.einsum(
        "hqk,qhd->khd", score_grad, query_split, preferred_element_type=jnp.float32
    )
    value_accum = jnp.einsum(
        "hqk,qhd->khd", weights.astype(jnp.bfloat16), grad_split, preferred_element_type=jnp.float32
    )
    key_accum, value_accum = (key_accum, value_accum)
    key_grad = (key_accum * scaling).astype(jnp.bfloat16).reshape(patches, columns)
    value_grad = value_accum.astype(jnp.bfloat16).reshape(patches, columns)
    return (query_grad, key_grad, value_grad)


def solution(mesh):
    in_specs = (
        P("wide", "narrow"),
        P("wide", "narrow"),
        P("wide", "narrow"),
        P(("wide", "narrow"), None),
        P(),
    )
    out_specs = (P("wide", "narrow"), P("wide", "narrow"), P("wide", "narrow"))
    return jax.shard_map(
        on_device, mesh=mesh, in_specs=in_specs, out_specs=out_specs, check_vma=False
    )
```

profile of v0, /device:TPU:0, one launch (start us, length us, event | category | flops | bytes accessed | tf_op | source)
XLA Modules:
  0.0 240.6 jit_solution(15646590345335519802)
XLA Ops:
  7.2 0.0 copy-start
  7.2 0.0 all-gather.7.cloned.1.call-start
  7.2 0.7 all-gather.7.cloned.1.call-update
  7.9 0.0 all-gather.9.cloned.1.call-start
  8.0 0.7 all-gather.9.cloned.1.call-update
  8.7 0.0 all-gather.11.cloned.1.call-start
  8.7 0.7 all-gather.11.cloned.1.call-update
  9.4 0.0 all-gather.13.cloned.1.call-start
  9.4 2.3 reshape.125
  11.7 1.4 copy.35
  13.1 13.4 %all_to_all.15 = bf16[20,2,4,2048]{3,2,0,1:T(4,128)(2,1)S(1)} all-to-all(bf16[20,2,4,2048]{3,2,0,1:T(4,128)(2,1)S(1)} %copy.35), channel_id=1, replica_groups=mesh['wide'=16,'narrow'=2] {'narrow'}, dimensions={1} | all-to-all | bytes 1310720 | tf_op jit(solution)/shard_map/all_to_all | solution.py:22
  26.6 0.0 copy-done
  26.6 1.5 fusion.25
  28.0 0.7 copy.67
  28.8 0.0 all-gather.13.cloned.1.call-update
  28.8 0.1 iota_compare_fusion.1
  28.9 0.1 iota_compare_fusion
  29.0 0.8 copy.37
  29.8 1.7 reshape_reshape.3
  31.5 30.6 %all-gather.7.cloned.1.call-done = bf16[640,3072]{1,0:T(8,128)(2,1)} async-done(((bf16[40,3072]{1,0:T(8,128)(2,1)}), bf16[640,3072]{1,0:T(8,128)(2,1)}) %all-gather.7.cloned.1.call-update) | async-done | bytes 3932176 | tf_op jit(solution)/shard_map/all_gather | solution.py:42
  62.1 6.3 %copy.32 = bf16[640,3072]{0,1:T(8,128)(2,1)} copy(bf16[640,3072]{1,0:T(8,128)(2,1)} %all-gather.7.cloned.1.call-done) | data formatting | bytes 7864320 | tf_op jit(solution)/shard_map/all_gather | solution.py:42
  68.4 0.0 copy-start.3
  68.4 43.6 %all-gather.9.cloned.1.call-done = bf16[640,3072]{1,0:T(8,128)(2,1)} async-done(((bf16[40,3072]{1,0:T(8,128)(2,1)}), bf16[640,3072]{1,0:T(8,128)(2,1)}) %all-gather.9.cloned.1.call-update) | async-done | bytes 3932176 | tf_op jit(solution)/shard_map/all_gather | solution.py:43
  112.0 6.2 %copy.38 = bf16[640,3072]{0,1:T(8,128)(2,1)} copy(bf16[640,3072]{1,0:T(8,128)(2,1)} %all-gather.9.cloned.1.call-done) | data formatting | bytes 7864320 | tf_op jit(solution)/shard_map/all_gather | solution.py:43
  118.3 0.0 copy-done.3
  118.3 0.0 copy-start.2
  118.3 3.3 %fusion.57 = (f32[24,40]{1,0:T(8,128)S(1)}, f32[24,40,640]{2,1,0:T(8,128)S(1)}) fusion(bf16[640,24,128]{0,2,1:T(8,128)(2,1)} %bitcast.76, pred[40,640]{1,0:T(8,128)(4,1)S(1)} %iota_compare_fusion.1, bf16[40,3072]{1,0:T(8,128)(2,1)S(1)} %copy-done.3), kind=kOutput, calls=%fused_computation.62 | convolution fusion | flops 159128640 | bytes 6664960 | tf_op jit(solution)/shard_map/qhd,khd->hqk/dot_general | solution.py:74
  121.6 0.2 copy-done.2
  121.8 0.0 copy-done.5
  121.8 1.4 fusion.2
  123.2 0.7 copy-done.1
  123.9 1.8 fusion.33
  125.7 0.7 copy.94
  126.4 19.6 %all-gather = f32[16,40,24]{1,2,0:T(8,128)S(1)} all-gather(f32[1,40,24]{1,2,0:T(8,128)S(1)} %bitcast.88), channel_id=1, replica_groups=mesh['wide'=16,'narrow'=2] {'wide'}, dimensions={0}, use_global_device_ids=true | all-gather | bytes 65280 | tf_op jit(solution)/shard_map/all_gather | solution.py:89
  146.1 0.1 reshape.137
  146.2 18.5 %all-gather.1 = f32[16,40,24]{1,2,0:T(8,128)S(1)} all-gather(f32[1,40,24]{1,2,0:T(8,128)S(1)} %bitcast.87), channel_id=1, replica_groups=mesh['wide'=16,'narrow'=2] {'wide'}, dimensions={0}, use_global_device_ids=true | all-gather | bytes 65280 | tf_op jit(solution)/shard_map/all_gather | solution.py:90
  164.7 0.1 reshape.139
  164.9 0.0 copy-start.4
  164.9 0.0 all-gather.11.cloned.1.call-done
  164.9 6.4 %copy.43 = bf16[640,3072]{0,1:T(8,128)(2,1)} copy(bf16[640,3072]{1,0:T(8,128)(2,1)} %all-gather.11.cloned.1.call-done) | data formatting | bytes 7864320 | tf_op jit(solution)/shard_map/all_gather | solution.py:92
  171.4 0.0 copy-done.4
  171.4 4.5 %fusion.43 = f32[24,640,40]{1,2,0:T(8,128)} fusion(bf16[640,24,128]{0,2,1:T(8,128)(2,1)} %bitcast.78, bf16[40,3072]{1,0:T(8,128)(2,1)S(1)} %copy-done.4), kind=kOutput, calls=%fused_computation.43 | convolution fusion | flops 157286400 | bytes 6635520 | tf_op jit(solution)/shard_map/qhd,khd->hqk/dot_general | solution.py:100
  175.9 37.4 %all-gather.13.cloned.1.call-done = bf16[640,3072]{1,0:T(8,128)(2,1)} async-done(((bf16[40,3072]{1,0:T(8,128)(2,1)}), bf16[640,3072]{1,0:T(8,128)(2,1)}) %all-gather.13.cloned.1.call-update) | async-done | bytes 3932176 | tf_op jit(solution)/shard_map/all_gather | solution.py:93
  213.3 6.3 %copy.48 = bf16[640,3072]{0,1:T(8,128)(2,1)} copy(bf16[640,3072]{1,0:T(8,128)(2,1)} %all-gather.13.cloned.1.call-done) | data formatting | bytes 7864320 | tf_op jit(solution)/shard_map/all_gather | solution.py:93
  219.6 5.3 %fusion.35 = bf16[24,5,8,128]{3,2,1,0:T(8,128)(2,1)} fusion(bf16[640,24,128]{0,2,1:T(8,128)(2,1)} %bitcast.81, f32[24,640,40]{1,2,0:T(8,128)} %fusion.43, f32[24,640]{1,0:T(8,128)S(1)} %bitcast.89, pred[640,40]{0,1:T(8,128)(4,1)S(1)} %iota_compare_fusion), kind=kOutput, calls=%fused_computation.36 | convolution fusion | flops 160481280 | bytes 6722560 | tf_op jit(solution)/shard_map/hqk,qhd->khd/dot_general | solution.py:112
  224.9 0.0 copy-done.6
  224.9 7.3 %fusion.34 = bf16[24,5,8,128]{3,2,1,0:T(8,128)(2,1)} fusion(bf16[640,24,128]{0,2,1:T(8,128)(2,1)} %bitcast.79, f32[24,640,40]{1,2,0:T(8,128)} %fusion.43, bf16[640,24,128]{0,2,1:T(8,128)(2,1)} %bitcast.82, f32[24,640]{1,0:T(8,128)S(1)} %bitcast.91, f32[24,640]{1,0:T(8,128)S(1)} %bitcast.90, pred[640,40]{0,1:T(8,128)(4,1)S(1)} %iota_compare_fusion, ...), kind=kOutput, calls=%fused_computation.35 | convolution fusion | flops 319119360 | bytes 10961920 | tf_op jit(solution)/shard_map/hqk,qhd->khd/dot_general | solution.py:109
  232.1 1.9 copy_bitcast_fusion
  (8 shorter events, 0.1 us)
Async XLA Ops:
  7.2 19.4 %copy-start = (bf16[768,2048]{1,0:T(8,128)(2,1)S(1)}, bf16[768,2048]{1,0:T(8,128)(2,1)}, u32[]{:S(2)}) copy-start(bf16[768,2048]{1,0:T(8,128)(2,1)} %param.9) | copy-start | bytes 9437188
  7.2 54.9 %all-gather.7.cloned.1.call-start = ((), (), s32[]{:S(2)}) async-start(), calls=%async_computation.1 | async-start | bytes 4177920 | tf_op jit(solution)/shard_map/all_gather | solution.py:42
  7.9 104.1 %all-gather.9.cloned.1.call-start = ((), (), s32[]{:S(2)}) async-start(), calls=%async_computation.2 | async-start | bytes 4177920 | tf_op jit(solution)/shard_map/all_gather | solution.py:43
  8.7 156.2 %all-gather.11.cloned.1.call-start = ((), (), s32[]{:S(2)}) async-start(), calls=%async_computation.3 | async-start | bytes 4177920 | tf_op jit(solution)/shard_map/all_gather | solution.py:92
  9.4 203.9 %all-gather.13.cloned.1.call-start = ((), (), s32[]{:S(2)}) async-start(), calls=%async_computation.4 | async-start | bytes 4177920 | tf_op jit(solution)/shard_map/all_gather | solution.py:93
  68.4 49.9 %copy-start.3 = (bf16[40,3072]{1,0:T(8,128)(2,1)S(1)}, bf16[40,3072]{1,0:T(8,128)(2,1)}, u32[]{:S(2)}) copy-start(bf16[40,3072]{1,0:T(8,128)(2,1)} %param.5) | copy-start | bytes 737284
  118.3 3.5 %copy-start.2 = (bf16[640,3072]{0,1:T(8,128)(2,1)S(1)}, bf16[640,3072]{0,1:T(8,128)(2,1)}, u32[]{:S(2)}) copy-start(bf16[640,3072]{0,1:T(8,128)(2,1)} %copy.38) | copy-start | bytes 11796484
  118.3 3.5 %copy-start.5 = (bf16[40,24,128]{2,1,0:T(8,128)(2,1)S(1)}, bf16[40,24,128]{2,1,0:T(8,128)(2,1)}, u32[]{:S(2)}) copy-start(bf16[40,24,128]{2,1,0:T(8,128)(2,1)} %reshape_reshape.3) | copy-start | bytes 737284
  121.8 2.1 copy-start.1
  164.9 6.5 %copy-start.4 = (bf16[40,3072]{1,0:T(8,128)(2,1)S(1)}, bf16[40,3072]{1,0:T(8,128)(2,1)}, u32[]{:S(2)}) copy-start(bf16[40,3072]{1,0:T(8,128)(2,1)} %param.6) | copy-start | bytes 737284
  219.6 5.3 %copy-start.6 = (bf16[40,3072]{1,0:T(8,128)(2,1)S(1)}, bf16[40,3072]{1,0:T(8,128)(2,1)}, u32[]{:S(2)}) copy-start(bf16[40,3072]{1,0:T(8,128)(2,1)} %param.7) | copy-start | bytes 737284
Sparse Core Ops, SparseCore 0:
  10.3 51.7 all-gather.6
  64.3 47.6 all-gather.8
  114.3 48.4 all-gather.10
  164.9 48.3 all-gather.12
where the time goes:
time: 241 us
  waiting for transfers between devices  114 us (47%)
  blocking collectives  51.5 us (21%)
  local copies, waits for them, and re-layouts  36.1 us (15%)
  matrix products  25 us (10%)
  between operations  13.9 us (6%)
    all_gather x1, waiting for transfers between devices, on_device(): lax.all_gather(value_rows, 'wide', axis=0, tiled=True)  43.6 us
    all_gather x1, waiting for transfers between devices, on_device(): grad_piece = lax.all_gather(incoming, 'wide', axis=0, tiled=True)  37.4 us
    all_gather x1, waiting for transfers between devices, on_device(): lax.all_gather(key_rows, 'wide', axis=0, tiled=True)  30.6 us
    all_gather x1, blocking collectives, on_device(): lax.all_gather(log_total, 'wide', axis=1, tiled=True)  19.6 us
    all_gather x1, blocking collectives, on_device(): lax.all_gather(row_delta, 'wide', axis=1, tiled=True)  18.5 us
    all_to_all x1, blocking collectives, on_device(): lax.all_to_all(grouped, 'narrow', split_axis=1, concat_axis=0, tiled=True)  13.4 us
    dot_general x1, matrix products, on_device(): jnp.einsum('hqk,qhd->khd', score_grad, query_split, preferred_element_typ...  7.27 us
    all_gather x1, local copies, waits for them, and re-layouts, on_device(): query_piece = lax.all_gather(query_rows, 'wide', axis=0, tiled=True)  6.45 us
  transfers between devices with their start and end apart: 4, of which 3 were waited for; matrix products, arithmetic and copies ran while one was open for 16% of the time, Pallas kernels for 0%

commit v1 on v0

--- a/solution.py
+++ b/solution.py
@@ -7,6 +7,18 @@
 HD = 128
 PATCH = 8
 lowest = -1e30
+
+
+def gather_by_bits(value, axis, dim):
+    ways, here = (lax.axis_size(axis), lax.axis_index(axis))
+    grown, reach = (value, 1)
+    while reach < ways:
+        theirs = lax.ppermute(grown, axis, [(d, d ^ reach) for d in range(ways)])
+        mine_first = jnp.concatenate([grown, theirs], axis=dim)
+        theirs_first = jnp.concatenate([theirs, grown], axis=dim)
+        grown = jnp.where(here & reach == 0, mine_first, theirs_first)
+        reach = 2 * reach
+    return grown
 
 
 def on_device(query_rows, key_rows, value_rows, mid_grad, link_weight):
@@ -40,7 +52,7 @@
     )
     pieces = (
         lax.all_gather(key_rows, "wide", axis=0, tiled=True),
-        lax.all_gather(value_rows, "wide", axis=0, tiled=True),
+        gather_by_bits(value_rows, "wide", 0),
     )
     key_piece, value_piece = pieces
     piece_rows = key_piece.shape[0]

time: 241 us -> 291 us (1.21)
  waiting for transfers between devices: 114 us -> 151 us
  other arithmetic: 0.19 us -> 13.4 us
  blocking collectives: 51.5 us -> 39.1 us
  starting transfers between devices: 0.15 us -> 10.2 us
    ppermute x0 -> x4, waiting for transfers between devices: none -> 139 us  [gather_by_bits(): theirs = lax.ppermute(grown, axis, [(d, d ^ reach) for d in range(ways)])]
    all_gather x1 -> x0, waiting for transfers between devices: 43.6 us -> none  [on_device(): lax.all_gather(value_rows, 'wide', axis=0, tiled=True)]
    all_gather x1, waiting for transfers between devices: 37.4 us -> 0.01 us  [on_device(): grad_piece = lax.all_gather(incoming, 'wide', axis=0, tiled=True)]
    all_gather x1, waiting for transfers between devices: 30.6 us -> 0.01 us  [on_device(): lax.all_gather(key_rows, 'wide', axis=0, tiled=True)]
    all_to_all x1 -> x0, blocking collectives: 13.4 us -> none  [on_device(): lax.all_to_all(grouped, 'narrow', split_axis=1, concat_axis=0, tiled=True)]
    select_n x0 -> x6, other arithmetic: none -> 13.2 us  [gather_by_bits(): grown = jnp.where(here & reach == 0, mine_first, theirs_first)]
    all_to_all x0 -> x1, waiting for transfers between devices: none -> 10.4 us  [on_device(): lax.all_to_all(grouped, 'narrow', split_axis=1, concat_axis=0, tiled=True)]
    concatenate x0 -> x5, local copies, waits for them, and re-layouts: none -> 6.9 us  [gather_by_bits(): mine_first = jnp.concatenate([grown, theirs], axis=dim)]
  transfers between devices with their start and end apart: 4 -> 8, of which waited for: 3 -> 4; matrix products, arithmetic and copies ran while one was open for 16% -> 19% of each run, Pallas kernels for 0% -> 0%
where the time goes in v1:
time: 291 us
  waiting for transfers between devices  151 us (52%)
  blocking collectives  39.1 us (13%)
  local copies, waits for them, and re-layouts  35.9 us (12%)
  matrix products  27.4 us (9%)
  between operations  13.9 us (5%)
  other arithmetic  13.4 us (5%)
  starting transfers between devices  10.2 us (4%)
    ppermute x4, waiting for transfers between devices, gather_by_bits(): theirs = lax.ppermute(grown, axis, [(d, d ^ reach) for d in range(ways)])  139 us
    all_gather x1, blocking collectives, on_device(): lax.all_gather(log_total, 'wide', axis=1, tiled=True)  20.8 us
    all_gather x1, blocking collectives, on_device(): lax.all_gather(row_delta, 'wide', axis=1, tiled=True)  18.3 us
    select_n x6, other arithmetic, gather_by_bits(): grown = jnp.where(here & reach == 0, mine_first, theirs_first)  13.2 us
    all_to_all x1, waiting for transfers between devices, on_device(): lax.all_to_all(grouped, 'narrow', split_axis=1, concat_axis=0, tiled=True)  10.4 us
    dot_general x1, matrix products, on_device(): jnp.einsum('hqk,qhd->khd', score_grad, query_split, preferred_element_typ...  7.29 us
    concatenate x5, local copies, waits for them, and re-layouts, gather_by_bits(): mine_first = jnp.concatenate([grown, theirs], axis=dim)  6.9 us
    all_gather x1, local copies, waits for them, and re-layouts, on_device(): query_piece = lax.all_gather(query_rows, 'wide', axis=0, tiled=True)  6.37 us
  transfers between devices with their start and end apart: 8, of which 4 were waited for; matrix products, arithmetic and copies ran while one was open for 19% of the time, Pallas kernels for 0%

profile of v1, /device:TPU:0, one launch (start us, length us, event | category | flops | bytes accessed | tf_op | source)
XLA Modules:
  0.0 290.5 jit_solution(10683717263414463698)
XLA Ops:
  7.2 0.7 all-gather.6.cloned.1.call-update
  7.9 0.0 all-gather.8.cloned.1.call-start
  8.0 0.7 all-gather.8.cloned.1.call-update
  8.7 2.4 reshape.137
  11.0 2.3 copy.53
  13.3 4.3 %all-to-all-start = ((bf16[20,2,4,2048]{3,2,0,1:T(4,128)(2,1)}), bf16[20,2,4,2048]{3,2,0,1:T(4,128)(2,1)}, u32[]{:S(2)}, u32[]{:S(2)}) async-start(bf16[20,2,4,2048]{3,2,0,1:T(4,128)(2,1)} %copy.53), calls=%async_computation | async-start | bytes 1310720 | tf_op jit(solution)/shard_map/all_to_all | solution.py:34
  17.6 0.0 all-gather.10.cloned.1.call-start
  17.7 0.6 collective-permute-start
  18.3 10.4 %all-to-all-done = bf16[20,2,4,2048]{3,2,0,1:T(4,128)(2,1)} async-done(((bf16[20,2,4,2048]{3,2,0,1:T(4,128)(2,1)}), bf16[20,2,4,2048]{3,2,0,1:T(4,128)(2,1)}, u32[]{:S(2)}, u32[]{:S(2)}) %all-to-all-start) | async-done | bytes 655392 | tf_op jit(solution)/shard_map/all_to_all | solution.py:34
  28.6 2.5 fusion.32
  31.1 0.7 copy-done.8
  31.8 0.7 copy.96
  32.6 2.0 maximum_select_fusion.7
  34.5 1.7 collective-permute-start.1
  36.2 18.5 %collective-permute-done.1 = bf16[80,3072]{1,0:T(8,128)(2,1)} collective-permute-done((bf16[80,3072]{1,0:T(8,128)(2,1)}, bf16[80,3072]{1,0:T(8,128)(2,1)}, u32[]{:S(2)}, u32[]{:S(2)}) %collective-permute-start.1) | collective-permute-done | bytes 491552 | tf_op jit(solution)/shard_map/ppermute | solution.py:16
  54.7 2.7 maximum_select_fusion.5
  57.5 1.5 collective-permute-start.2
  58.9 24.6 %collective-permute-done.2 = bf16[160,3072]{1,0:T(8,128)(2,1)} collective-permute-done((bf16[160,3072]{1,0:T(8,128)(2,1)}, bf16[160,3072]{1,0:T(8,128)(2,1)}, u32[]{:S(2)}, u32[]{:S(2)}) %collective-permute-start.2) | collective-permute-done | bytes 983072 | tf_op jit(solution)/shard_map/ppermute | solution.py:16
  83.5 4.2 %maximum_select_fusion.3 = bf16[320,3072]{1,0:T(8,128)(2,1)} fusion(bf16[160,3072]{1,0:T(8,128)(2,1)} %collective-permute-done.2, bf16[160,3072]{1,0:T(8,128)(2,1)} %maximum_select_fusion.5, pred[]{:T(512)S(6)} %eq.13), kind=kLoop, calls=%fused_computation.19 | loop fusion | flops 8847360 | bytes 3932161 | tf_op jit(solution)/shard_map/jit(_where)/select_n | solution.py:19
  87.8 2.1 collective-permute-start.3
  89.8 0.1 iota_compare_fusion.1
  89.9 0.1 iota_compare_fusion
  90.1 1.0 copy_bitcast_fusion.6
  91.1 0.9 maximum_select_fusion.6
  92.0 0.1 copy.55
  92.1 0.8 reshape_reshape.3
  92.9 1.1 copy_bitcast_fusion.2
  94.0 1.5 maximum_select_fusion.4
  95.5 1.4 copy_bitcast_fusion.1
  96.8 1.9 maximum_select_fusion.2
  98.7 95.7 %collective-permute-done.3 = bf16[320,3072]{1,0:T(8,128)(2,1)} collective-permute-done((bf16[320,3072]{1,0:T(8,128)(2,1)}, bf16[320,3072]{1,0:T(8,128)(2,1)}, u32[]{:S(2)}, u32[]{:S(2)}) %collective-permute-start.3) | collective-permute-done | bytes 1966112 | tf_op jit(solution)/shard_map/ppermute | solution.py:16
  194.4 3.4 %copy_bitcast_fusion = bf16[320,24,128]{2,0,1:T(8,128)(2,1)} fusion(bf16[320,3072]{1,0:T(8,128)(2,1)} %collective-permute-done.3), kind=kLoop, calls=%fused_computation.17 | loop fusion | bytes 3932160 | tf_op jit(solution)/shard_map/concatenate | solution.py:17
  197.7 6.3 %copy.50 = bf16[640,3072]{0,1:T(8,128)(2,1)} copy(bf16[640,3072]{1,0:T(8,128)(2,1)} %all-gather.6.cloned.1.call-done) | data formatting | bytes 7864320 | tf_op jit(solution)/shard_map/all_gather | solution.py:54
  204.1 3.3 %fusion.60 = (f32[24,40]{1,0:T(8,128)S(1)}, f32[24,40,640]{2,1,0:T(8,128)S(1)}) fusion(bf16[640,24,128]{0,2,1:T(8,128)(2,1)} %bitcast.96, pred[40,640]{1,0:T(8,128)(4,1)S(1)} %iota_compare_fusion.1, bf16[40,3072]{1,0:T(8,128)(2,1)S(1)} %copy-done.4), kind=kOutput, calls=%fused_computation.79 | convolution fusion | flops 159128640 | bytes 6664960 | tf_op jit(solution)/shard_map/qhd,khd->hqk/dot_general | solution.py:86
  207.5 0.2 copy-done.3
  207.6 2.8 fusion.9
  210.5 1.8 fusion.40
  212.3 0.7 copy.125
  213.0 20.8 %all-gather = f32[16,40,24]{1,2,0:T(8,128)S(1)} all-gather(f32[1,40,24]{1,2,0:T(8,128)S(1)} %bitcast.106), channel_id=1, replica_groups=mesh['wide'=16,'narrow'=2] {'wide'}, dimensions={0}, use_global_device_ids=true | all-gather | bytes 65280 | tf_op jit(solution)/shard_map/all_gather | solution.py:101
  233.9 0.1 reshape.147
  234.0 18.3 %all-gather.1 = f32[16,40,24]{1,2,0:T(8,128)S(1)} all-gather(f32[1,40,24]{1,2,0:T(8,128)S(1)} %bitcast.105), channel_id=1, replica_groups=mesh['wide'=16,'narrow'=2] {'wide'}, dimensions={0}, use_global_device_ids=true | all-gather | bytes 65280 | tf_op jit(solution)/shard_map/all_gather | solution.py:102
  252.4 0.1 reshape.149
  252.5 6.4 %copy.69 = bf16[640,3072]{0,1:T(8,128)(2,1)} copy(bf16[640,3072]{1,0:T(8,128)(2,1)} %all-gather.8.cloned.1.call-done) | data formatting | bytes 7864320 | tf_op jit(solution)/shard_map/all_gather | solution.py:104
  258.9 4.3 %fusion.46 = f32[24,640,40]{1,2,0:T(8,128)} fusion(bf16[640,24,128]{0,2,1:T(8,128)(2,1)} %bitcast.98, bf16[40,3072]{1,0:T(8,128)(2,1)S(1)} %copy-done.5), kind=kOutput, calls=%fused_computation.58 | convolution fusion | flops 157286400 | bytes 6635520 | tf_op jit(solution)/shard_map/qhd,khd->hqk/dot_general | solution.py:112
  263.3 6.2 %copy.74 = bf16[640,3072]{0,1:T(8,128)(2,1)} copy(bf16[640,3072]{1,0:T(8,128)(2,1)} %all-gather.10.cloned.1.call-done) | data formatting | bytes 7864320 | tf_op jit(solution)/shard_map/all_gather | solution.py:105
  269.5 5.3 %fusion.42 = bf16[24,5,8,128]{3,2,1,0:T(8,128)(2,1)} fusion(bf16[640,24,128]{0,2,1:T(8,128)(2,1)} %bitcast.100, f32[24,640,40]{1,2,0:T(8,128)} %fusion.46, f32[24,640]{1,0:T(8,128)S(1)} %bitcast.107, pred[640,40]{0,1:T(8,128)(4,1)S(1)} %iota_compare_fusion), kind=kOutput, calls=%fused_computation.47 | convolution fusion | flops 160481280 | bytes 6722560 | tf_op jit(solution)/shard_map/hqk,qhd->khd/dot_general | solution.py:124
  274.8 7.3 %fusion.41 = bf16[24,5,8,128]{3,2,1,0:T(8,128)(2,1)} fusion(bf16[640,24,128]{0,2,1:T(8,128)(2,1)} %bitcast.99, f32[24,640,40]{1,2,0:T(8,128)} %fusion.46, bf16[640,24,128]{0,2,1:T(8,128)(2,1)} %bitcast.101, f32[24,640]{1,0:T(8,128)S(1)} %bitcast.109, f32[24,640]{1,0:T(8,128)S(1)} %bitcast.108, pred[640,40]{0,1:T(8,128)(4,1)S(1)} %iota_compare_fusion, ...), kind=kOutput, calls=%fused_computation.46 | convolution fusion | flops 319119360 | bytes 10961920 | tf_op jit(solution)/shard_map/hqk,qhd->khd/dot_general | solution.py:121
  282.1 1.9 copy_bitcast_fusion.3
  (32 shorter events, 0.3 us)
Async XLA Ops:
  7.2 21.5 %copy-start = (bf16[768,2048]{1,0:T(8,128)(2,1)S(1)}, bf16[768,2048]{1,0:T(8,128)(2,1)}, u32[]{:S(2)}) copy-start(bf16[768,2048]{1,0:T(8,128)(2,1)} %param.9) | copy-start | bytes 9437188
  7.2 10.5 %copy-start.6 = (bf16[40,3072]{1,0:T(8,128)(2,1)S(1)}, bf16[40,3072]{1,0:T(8,128)(2,1)}, u32[]{:S(2)}) copy-start(bf16[40,3072]{1,0:T(8,128)(2,1)} %param.7) | copy-start | bytes 737284
  7.2 190.5 %all-gather.6.cloned.1.call-start = ((), (), s32[]{:S(2)}) async-start(), calls=%async_computation.1 | async-start | bytes 4177920 | tf_op jit(solution)/shard_map/all_gather | solution.py:54
  7.9 244.6 %all-gather.8.cloned.1.call-start = ((), (), s32[]{:S(2)}) async-start(), calls=%async_computation.2 | async-start | bytes 4177920 | tf_op jit(solution)/shard_map/all_gather | solution.py:104
  13.3 15.3 %all-to-all-start = ((bf16[20,2,4,2048]{3,2,0,1:T(4,128)(2,1)}), bf16[20,2,4,2048]{3,2,0,1:T(4,128)(2,1)}, u32[]{:S(2)}, u32[]{:S(2)}) async-start(bf16[20,2,4,2048]{3,2,0,1:T(4,128)(2,1)} %copy.53), calls=%async_computation | async-start | bytes 1310720 | tf_op jit(solution)/shard_map/all_to_all | solution.py:34
  17.6 245.6 %all-gather.10.cloned.1.call-start = ((), (), s32[]{:S(2)}) async-start(), calls=%async_computation.3 | async-start | bytes 4177920 | tf_op jit(solution)/shard_map/all_gather | solution.py:105
  17.7 14.9 %collective-permute-start = (bf16[40,3072]{1,0:T(8,128)(2,1)S(1)}, bf16[40,3072]{1,0:T(8,128)(2,1)}, u32[]{:S(2)}, u32[]{:S(2)}) collective-permute-start(bf16[40,3072]{1,0:T(8,128)(2,1)S(1)} %copy-done.6), channel_id=1, source_target_pairs={{0,2},{2,0},{4,6},{6,4},{8,10},{10,8},{12,14},{14,12},{16,18},{18,... | collective-permute-start | bytes 737288 | tf_op jit(solution)/shard_map/ppermute | solution.py:16
  31.1 0.7 copy-start.8
  34.5 20.2 %collective-permute-start.1 = (bf16[80,3072]{1,0:T(8,128)(2,1)}, bf16[80,3072]{1,0:T(8,128)(2,1)}, u32[]{:S(2)}, u32[]{:S(2)}) collective-permute-start(bf16[80,3072]{1,0:T(8,128)(2,1)} %maximum_select_fusion.7), channel_id=1, source_target_pairs={{0,4},{2,6},{4,0},{6,2},{8,12},{10,14},{12,8},{14,10},{16,20},{18,... | collective-permute-start | bytes 1474568 | tf_op jit(solution)/shard_map/ppermute | solution.py:16
  57.5 26.1 %collective-permute-start.2 = (bf16[160,3072]{1,0:T(8,128)(2,1)}, bf16[160,3072]{1,0:T(8,128)(2,1)}, u32[]{:S(2)}, u32[]{:S(2)}) collective-permute-start(bf16[160,3072]{1,0:T(8,128)(2,1)} %maximum_select_fusion.5), channel_id=1, source_target_pairs={{0,8},{2,10},{4,12},{6,14},{8,0},{10,2},{12,4},{14,6},{16,24},{18,... | collective-permute-start | bytes 2949128 | tf_op jit(solution)/shard_map/ppermute | solution.py:16
  58.9 33.0 %copy-start.9 = (bf16[40,4,768]{2,0,1:T(8,128)(2,1)S(1)}, bf16[40,4,768]{2,0,1:T(8,128)(2,1)}, u32[]{:S(2)}) copy-start(bf16[40,4,768]{2,0,1:T(8,128)(2,1)} %copy-done.8) | copy-start | bytes 737284
  87.8 106.6 %collective-permute-start.3 = (bf16[320,3072]{1,0:T(8,128)(2,1)}, bf16[320,3072]{1,0:T(8,128)(2,1)}, u32[]{:S(2)}, u32[]{:S(2)}) collective-permute-start(bf16[320,3072]{1,0:T(8,128)(2,1)} %maximum_select_fusion.3), channel_id=1, source_target_pairs={{0,16},{2,18},{4,20},{6,22},{8,24},{10,26},{12,28},{14,30},{16,0},... | collective-permute-start | bytes 5898248 | tf_op jit(solution)/shard_map/ppermute | solution.py:16
  197.7 6.3 %copy-start.4 = (bf16[40,3072]{1,0:T(8,128)(2,1)S(1)}, bf16[40,3072]{1,0:T(8,128)(2,1)}, u32[]{:S(2)}) copy-start(bf16[40,3072]{1,0:T(8,128)(2,1)} %param.5) | copy-start | bytes 737284
  204.1 3.4 %copy-start.2 = (bf16[320,24,128]{2,0,1:T(8,128)(2,1)S(1)}, bf16[320,24,128]{2,0,1:T(8,128)(2,1)}, u32[]{:S(2)}) copy-start(bf16[320,24,128]{2,0,1:T(8,128)(2,1)} %maximum_select_fusion.2) | copy-start | bytes 5898244
  204.1 3.5 %copy-start.3 = (bf16[320,24,128]{2,0,1:T(8,128)(2,1)S(1)}, bf16[320,24,128]{2,0,1:T(8,128)(2,1)}, u32[]{:S(2)}) copy-start(bf16[320,24,128]{2,0,1:T(8,128)(2,1)} %copy_bitcast_fusion) | copy-start | bytes 5898244
  204.1 3.5 %copy-start.10 = (bf16[40,24,128]{2,1,0:T(8,128)(2,1)S(1)}, bf16[40,24,128]{2,1,0:T(8,128)(2,1)}, u32[]{:S(2)}) copy-start(bf16[40,24,128]{2,1,0:T(8,128)(2,1)} %reshape_reshape.3) | copy-start | bytes 737284
  207.6 2.9 copy-start.1
  252.5 6.4 %copy-start.5 = (bf16[40,3072]{1,0:T(8,128)(2,1)S(1)}, bf16[40,3072]{1,0:T(8,128)(2,1)}, u32[]{:S(2)}) copy-start(bf16[40,3072]{1,0:T(8,128)(2,1)} %param.6) | copy-start | bytes 737284
  269.5 5.4 %copy-start.7 = (bf16[40,3072]{1,0:T(8,128)(2,1)S(1)}, bf16[40,3072]{1,0:T(8,128)(2,1)}, u32[]{:S(2)}) copy-start(bf16[40,3072]{1,0:T(8,128)(2,1)} %param.7) | copy-start | bytes 737284
Sparse Core Ops, SparseCore 0:
  10.3 59.9 all-gather.5
  72.6 99.4 all-gather.7
  174.9 73.0 all-gather.9
